TPU v7x, 32 devices: a whole 2x2x4 slice. The times are simulated.
32 devices in a mesh: dp: 8 (over y, x, core), tensor: 4 (over z).
Axes of the slice: x: 2, y: 2, z: 4, core: 2. Of those that a mesh axis runs over, the one named last changes fastest.
Arguments:
- teacher_input: bfloat16 [8, 1024, 1280], P('dp', 'tensor'), may hold values from -6 to 6
- teacher_upstream: bfloat16 [8, 1024, 1280], P('dp', 'tensor'), may hold values from -6 to 6
- teacher_attn_gain: bfloat16 [1280], P('dp'), may hold values from 0.25 to 1.75
- teacher_attn_shift: bfloat16 [1280], P('dp'), may hold values from -1.75 to 1.75
- teacher_qkv_weight: bfloat16 [3, 1280, 1536], P(None, 'dp', 'tensor'), may hold values from -0.15625 to 0.15625
- teacher_qv_bias: bfloat16 [2, 1536], P(None, 'tensor'), may hold values from -0.625 to 0.625
- teacher_out_weight: bfloat16 [1536, 1280], P('tensor', 'dp'), may hold values from -1.25 to 1.25
- teacher_out_bias: bfloat16 [1280], P('dp'), may hold values from -1.75 to 1.75
- teacher_mlp_gain: bfloat16 [1280], P('dp'), may hold values from 0.25 to 1.75
- teacher_mlp_shift: bfloat16 [1280], P('dp'), may hold values from -1.75 to 1.75
- teacher_fc_weight: bfloat16 [1280, 5120], P('dp', 'tensor'), may hold values from -0.15625 to 0.15625
- teacher_fc_bias: bfloat16 [5120], P('tensor'), may hold values from -1.75 to 1.75
- teacher_proj_weight: bfloat16 [5120, 1280], P('tensor', 'dp'), may hold values from -0.078125 to 0.078125
- teacher_proj_bias: bfloat16 [1280], P('dp'), may hold values from -1.75 to 1.75
- student_input: bfloat16 [8, 1024, 768], P('dp', 'tensor'), may hold values from -6 to 6
- student_upstream: bfloat16 [8, 1024, 768], P('dp', 'tensor'), may hold values from -6 to 6
- student_attn_gain: bfloat16 [768], P('dp'), may hold values from 0.25 to 1.75
- student_attn_shift: bfloat16 [768], P('dp'), may hold values from -1.75 to 1.75
- student_qkv_weight: bfloat16 [3, 768, 768], P(None, 'dp', 'tensor'), may hold values from -0.21875 to 0.21875
- student_qv_bias: bfloat16 [2, 768], P(None, 'tensor'), may hold values from -0.625 to 0.625
- student_out_weight: bfloat16 [768, 768], P('tensor', 'dp'), may hold values from -1.75 to 1.75
- student_out_bias: bfloat16 [768], P('dp'), may hold values from -1.75 to 1.75
- student_mlp_gain: bfloat16 [768], P('dp'), may hold values from 0.25 to 1.75
- student_mlp_shift: bfloat16 [768], P('dp'), may hold values from -1.75 to 1.75
- student_fc_weight: bfloat16 [768, 3072], P('dp', 'tensor'), may hold values from -0.21875 to 0.21875
- student_fc_bias: bfloat16 [3072], P('tensor'), may hold values from -1.75 to 1.75
- student_proj_weight: bfloat16 [3072, 768], P('tensor', 'dp'), may hold values from -0.109375 to 0.109375
- student_proj_bias: bfloat16 [768], P('dp'), may hold values from -1.75 to 1.75
- span_starts: int32 [8], P('dp'), may hold values from 0 to 768, as said below
- head_slots: int32 [24], P('tensor'), may hold values from 0 to 1, as said below
Outputs:
- teacher_output: bfloat16 [8, 1024, 1280], P('dp', 'tensor')
- teacher_input_grad: bfloat16 [8, 1024, 1280], P('dp', 'tensor')
- teacher_attn_gain_grad: float32 [1280], P('dp')
- teacher_attn_shift_grad: float32 [1280], P('dp')
- teacher_qkv_weight_grad: float32 [3, 1280, 1536], P(None, 'dp', 'tensor')
- teacher_qv_bias_grad: float32 [2, 1536], P(None, 'tensor')
- teacher_out_weight_grad: float32 [1536, 1280], P('tensor', 'dp')
- teacher_out_bias_grad: float32 [1280], P('dp')
- teacher_mlp_gain_grad: float32 [1280], P('dp')
- teacher_mlp_shift_grad: float32 [1280], P('dp')
- teacher_fc_weight_grad: float32 [1280, 5120], P('dp', 'tensor')
- teacher_fc_bias_grad: float32 [5120], P('tensor')
- teacher_proj_weight_grad: float32 [5120, 1280], P('tensor', 'dp')
- teacher_proj_bias_grad: float32 [1280], P('dp')
- student_output: bfloat16 [8, 1024, 768], P('dp', 'tensor')
- student_input_grad: bfloat16 [8, 1024, 768], P('dp', 'tensor')
- student_attn_gain_grad: float32 [768], P('dp')
- student_attn_shift_grad: float32 [768], P('dp')
- student_qkv_weight_grad: float32 [3, 768, 768], P(None, 'dp', 'tensor')
- student_qv_bias_grad: float32 [2, 768], P(None, 'tensor')
- student_out_weight_grad: float32 [768, 768], P('tensor', 'dp')
- student_out_bias_grad: float32 [768], P('dp')
- student_mlp_gain_grad: float32 [768], P('dp')
- student_mlp_shift_grad: float32 [768], P('dp')
- student_fc_weight_grad: float32 [768, 3072], P('dp', 'tensor')
- student_fc_bias_grad: float32 [3072], P('tensor')
- student_proj_weight_grad: float32 [3072, 768], P('tensor', 'dp')
- student_proj_bias_grad: float32 [768], P('dp')
Inputs may be any that keep to these rules, and one draw needn't show every extreme that they name: `span_starts`: some sequence starts its span at 0 and some at 768. `head_slots`: exactly 20 of the 24 slots are 1.
All inputs are finite; a program needn't handle non-finite values.
Results may differ from a plain program's by a relative error of at most 0.02.
Values may be sent and summed in bfloat16 or wider, within the bound.
No kernel may reach another device: no remote copies, remote signals or barrier semaphores. Data moves between devices by JAX's collectives and lax.ppermute only.
A program may use at most 256 MiB of HBM per device.

v0:
```python
import jax
import jax.numpy as jnp
from jax import lax
from jax.sharding import PartitionSpec as P

HD = 64
SPAN = 256
epsilon = 1e-05
negative = -1e30


def layer_norm(values, norm_gain, norm_shift):
    center = values - jnp.mean(values, axis=-1, keepdims=True)
    spread = jnp.mean(center * center, axis=-1, keepdims=True)
    return center * lax.rsqrt(spread + epsilon) * norm_gain + norm_shift


def gelu_tanh(values):
    return jax.nn.gelu(values, approximate=True)


def visibility(first_row, block_rows, length, span_start):
    query_pos = first_row + jnp.arange(block_rows, dtype=jnp.int32)
    key_pos = jnp.arange(length, dtype=jnp.int32)
    query_in = (query_pos >= span_start) & (query_pos < span_start + SPAN)
    key_in = (key_pos >= span_start) & (key_pos < span_start + SPAN)
    return (key_pos[None, :] <= query_pos[:, None]) | query_in[:, None] & key_in[None, :]


def block_scores(query_block, key_rows, visible, score_scale):
    scores = (
        jnp.einsum("qhe,khe->hqk", query_block, key_rows, preferred_element_type=jnp.float32)
        * score_scale
    )
    return jnp.where(visible[None], scores, negative)


def attention_forward(query_rows, key_rows, value_rows, span_start, block_rows, score_scale):
    length = query_rows.shape[0]
    results = []
    log_sums = []
    for block_index in range(length // block_rows):
        first_row = block_index * block_rows
        visible = visibility(first_row, block_rows, length, span_start)
        scores = block_scores(
            query_rows[first_row : first_row + block_rows], key_rows, visible, score_scale
        )
        row_peak = jnp.max(scores, axis=-1, keepdims=True)
        raised = jnp.exp(scores - row_peak)
        row_total = jnp.sum(raised, axis=-1, keepdims=True)
        weights = (raised / row_total).astype(jnp.bfloat16)
        results.append(
            jnp.einsum("hqk,khe->qhe", weights, value_rows, preferred_element_type=jnp.float32)
        )
        log_sums.append(row_peak + jnp.log(row_total))
    return (jnp.concatenate(results, axis=0), log_sums)


def attention_backward(
    query_rows, key_rows, value_rows, log_sums, heads_grad, span_start, block_rows, score_scale
):
    length = query_rows.shape[0]
    query_grads = []
    key_grad = jnp.zeros(key_rows.shape, jnp.float32)
    value_grad = jnp.zeros(value_rows.shape, jnp.float32)
    for block_index in range(length // block_rows):
        first_row = block_index * block_rows
        last_row = first_row + block_rows
        visible = visibility(first_row, block_rows, length, span_start)
        scores = block_scores(query_rows[first_row:last_row], key_rows, visible, score_scale)
        probability = jnp.exp(scores - log_sums[block_index])
        grad_block = heads_grad[first_row:last_row]
        value_grad = value_grad + jnp.einsum(
            "hqk,qhe->khe",
            probability.astype(jnp.bfloat16),
            grad_block,
            preferred_element_type=jnp.float32,
        )
        prob_grad = jnp.einsum(
            "qhe,khe->hqk", grad_block, value_rows, preferred_element_type=jnp.float32
        )
        weighted = jnp.sum(probability * prob_grad, axis=-1, keepdims=True)
        score_grad = (probability * (prob_grad - weighted)).astype(jnp.bfloat16)
        query_grads.append(
            jnp.einsum("hqk,khe->qhe", score_grad, key_rows, preferred_element_type=jnp.float32)
            * score_scale
        )
        key_grad = (
            key_grad
            + jnp.einsum(
                "hqk,qhe->khe",
                score_grad,
                query_rows[first_row:last_row],
                preferred_element_type=jnp.float32,
            )
            * score_scale
        )
    return (jnp.concatenate(query_grads, axis=0), key_grad, value_grad)


def gather_rows(normed):
    return lax.all_gather(normed, "tensor", axis=0, tiled=True)


def gather_grads(branch_grad):
    return lax.all_gather(branch_grad, "tensor", axis=0, tiled=True)


def sum_rows(left_rows, right_weight):
    return lax.psum_scatter(
        jnp.dot(left_rows, right_weight, preferred_element_type=jnp.float32).astype(jnp.bfloat16),
        "tensor",
        scatter_dimension=0,
        tiled=True,
    ).astype(jnp.float32)


def back_rows(grad_stack, weight_stack):
    return lax.psum_scatter(
        jnp.einsum(
            "sle,sde->ld", grad_stack, weight_stack, preferred_element_type=jnp.float32
        ).astype(jnp.bfloat16),
        "tensor",
        scatter_dimension=0,
        tiled=True,
    ).astype(jnp.float32)


def run_block(
    inputs,
    upstream,
    attn_gain,
    attn_shift,
    qkv_weight,
    qv_bias,
    out_weight,
    out_bias,
    mlp_gain,
    mlp_shift,
    fc_weight,
    fc_bias,
    proj_weight,
    proj_bias,
    span_start,
    head_keep,
):
    gathered = (
        lax.all_gather(qkv_weight, "dp", axis=1, tiled=True),
        lax.all_gather(out_weight, "dp", axis=1, tiled=True),
        lax.all_gather(fc_weight, "dp", axis=0, tiled=True),
        lax.all_gather(proj_weight, "dp", axis=1, tiled=True),
        lax.all_gather(attn_gain, "dp", axis=0, tiled=True),
        lax.all_gather(attn_shift, "dp", axis=0, tiled=True),
        lax.all_gather(out_bias, "dp", axis=0, tiled=True),
        lax.all_gather(mlp_gain, "dp", axis=0, tiled=True),
        lax.all_gather(mlp_shift, "dp", axis=0, tiled=True),
        lax.all_gather(proj_bias, "dp", axis=0, tiled=True),
    )
    qkv_full, out_full, fc_full, proj_full = (gathered[0], gathered[1], gathered[2], gathered[3])
    gain_one = gathered[4].astype(jnp.float32)
    shift_one = gathered[5].astype(jnp.float32)
    bias_out = gathered[6].astype(jnp.float32)
    gain_two = gathered[7].astype(jnp.float32)
    shift_two = gathered[8].astype(jnp.float32)
    bias_proj = gathered[9].astype(jnp.float32)
    rows_first = inputs[0].astype(jnp.float32)
    normed, norm_back_one = jax.vjp(layer_norm, rows_first, gain_one, shift_one)
    normed_all = gather_rows(normed.astype(jnp.bfloat16))
    projected = jnp.einsum("ld,tde->tle", normed_all, qkv_full, preferred_element_type=jnp.float32)
    bias_pair = qv_bias.astype(jnp.float32)
    length = normed_all.shape[0]
    head_count = head_keep.shape[0]
    head_split = (length, head_count, HD)
    query_rows = (projected[0] + bias_pair[0]).astype(jnp.bfloat16).reshape(head_split)
    key_rows = projected[1].astype(jnp.bfloat16).reshape(head_split)
    value_rows = (projected[2] + bias_pair[1]).astype(jnp.bfloat16).reshape(head_split)
    block_rows = min(512, length)
    score_scale = 1.0 / HD**0.5
    attended, log_sums = attention_forward(
        query_rows, key_rows, value_rows, span_start, block_rows, score_scale
    )
    keep_float = head_keep.astype(jnp.float32)[None, :, None]
    heads_low = (attended * keep_float).astype(jnp.bfloat16).reshape(length, head_count * HD)
    attn_sum = sum_rows(heads_low, out_full)
    middle = rows_first + (attn_sum + bias_out)
    normed_two, norm_back_two = jax.vjp(layer_norm, middle, gain_two, shift_two)
    normed_two_all = gather_rows(normed_two.astype(jnp.bfloat16))
    hidden_pre = jnp.dot(
        normed_two_all, fc_full, preferred_element_type=jnp.float32
    ) + fc_bias.astype(jnp.float32)
    hidden, gelu_back = jax.vjp(gelu_tanh, hidden_pre)
    hidden_low = hidden.astype(jnp.bfloat16)
    mlp_sum = sum_rows(hidden_low, proj_full)
    result = middle + (mlp_sum + bias_proj)
    outputs = result.astype(jnp.bfloat16)[None]
    grad_result = upstream[0].astype(jnp.float32)
    grad_mlp_all = gather_grads(upstream[0])
    proj_bias_grad = jnp.sum(grad_mlp_all, axis=0, dtype=jnp.float32)
    proj_grad = jnp.einsum(
        "lf,ld->fd", hidden_low, grad_mlp_all, preferred_element_type=jnp.float32
    )
    hidden_grad = jnp.einsum(
        "ld,fd->lf", grad_mlp_all, proj_full, preferred_element_type=jnp.float32
    )
    pre_grad = gelu_back(hidden_grad)[0].astype(jnp.bfloat16)
    fc_bias_grad = jnp.sum(pre_grad, axis=0, dtype=jnp.float32)
    fc_grad = jnp.einsum("ld,lf->df", normed_two_all, pre_grad, preferred_element_type=jnp.float32)
    normed_two_grad = back_rows(pre_grad[None], fc_full[None])
    middle_from_norm, gain_two_grad, shift_two_grad = norm_back_two(normed_two_grad)
    middle_grad = grad_result + middle_from_norm
    grad_attn_all = gather_grads(middle_grad.astype(jnp.bfloat16))
    out_bias_grad = jnp.sum(grad_attn_all, axis=0, dtype=jnp.float32)
    out_grad = jnp.einsum("le,ld->ed", heads_low, grad_attn_all, preferred_element_type=jnp.float32)
    heads_grad = (
        jnp.einsum("ld,ed->le", grad_attn_all, out_full, preferred_element_type=jnp.float32)
        .astype(jnp.bfloat16)
        .reshape(head_split)
    )
    heads_grad = heads_grad * head_keep.astype(jnp.bfloat16)[None, :, None]
    query_grad, key_grad, value_grad = attention_backward(
        query_rows, key_rows, value_rows, log_sums, heads_grad, span_start, block_rows, score_scale
    )
    qkv_low = jnp.stack(
        [
            query_grad.reshape(length, head_count * HD),
            key_grad.reshape(length, head_count * HD),
            value_grad.reshape(length, head_count * HD),
        ]
    ).astype(jnp.bfloat16)
    qv_bias_grad = jnp.stack(
        [
            jnp.sum(qkv_low[0], axis=0, dtype=jnp.float32),
            jnp.sum(qkv_low[2], axis=0, dtype=jnp.float32),
        ]
    )
    qkv_grad = jnp.einsum("ld,tle->tde", normed_all, qkv_low, preferred_element_type=jnp.float32)
    normed_grad = back_rows(qkv_low, qkv_full)
    rows_from_norm, gain_one_grad, shift_one_grad = norm_back_one(normed_grad)
    input_grad = (middle_grad + rows_from_norm).astype(jnp.bfloat16)[None]
    norm_sums = lax.psum((gain_one_grad, shift_one_grad, gain_two_grad, shift_two_grad), "tensor")
    matrices = (
        qkv_grad,
        out_grad,
        fc_grad,
        proj_grad,
        norm_sums[0],
        norm_sums[1],
        out_bias_grad,
        norm_sums[2],
        norm_sums[3],
        proj_bias_grad,
    )
    biases = (qv_bias_grad, fc_bias_grad)
    return (outputs, input_grad, matrices, biases)


def arrange(outputs, input_grad, matrices, biases):
    return (
        outputs,
        input_grad,
        matrices[4],
        matrices[5],
        matrices[0],
        biases[0],
        matrices[1],
        matrices[6],
        matrices[7],
        matrices[8],
        matrices[2],
        biases[1],
        matrices[3],
        matrices[9],
    )


def on_device(
    teacher_input,
    teacher_upstream,
    teacher_attn_gain,
    teacher_attn_shift,
    teacher_qkv_weight,
    teacher_qv_bias,
    teacher_out_weight,
    teacher_out_bias,
    teacher_mlp_gain,
    teacher_mlp_shift,
    teacher_fc_weight,
    teacher_fc_bias,
    teacher_proj_weight,
    teacher_proj_bias,
    student_input,
    student_upstream,
    student_attn_gain,
    student_attn_shift,
    student_qkv_weight,
    student_qv_bias,
    student_out_weight,
    student_out_bias,
    student_mlp_gain,
    student_mlp_shift,
    student_fc_weight,
    student_fc_bias,
    student_proj_weight,
    student_proj_bias,
    span_starts,
    head_slots,
):
    span_start = span_starts[0]
    teacher = run_block(
        teacher_input,
        teacher_upstream,
        teacher_attn_gain,
        teacher_attn_shift,
        teacher_qkv_weight,
        teacher_qv_bias,
        teacher_out_weight,
        teacher_out_bias,
        teacher_mlp_gain,
        teacher_mlp_shift,
        teacher_fc_weight,
        teacher_fc_bias,
        teacher_proj_weight,
        teacher_proj_bias,
        span_start,
        head_slots,
    )
    student_keep = jnp.ones((student_qv_bias.shape[1] // HD,), jnp.int32)
    student = run_block(
        student_input,
        student_upstream,
        student_attn_gain,
        student_attn_shift,
        student_qkv_weight,
        student_qv_bias,
        student_out_weight,
        student_out_bias,
        student_mlp_gain,
        student_mlp_shift,
        student_fc_weight,
        student_fc_bias,
        student_proj_weight,
        student_proj_bias,
        span_start,
        student_keep,
    )
    teach_parts = teacher[2]
    learn_parts = student[2]
    summed = (
        lax.psum_scatter(teach_parts[0], "dp", scatter_dimension=1, tiled=True),
        lax.psum_scatter(teach_parts[1], "dp", scatter_dimension=1, tiled=True),
        lax.psum_scatter(teach_parts[2], "dp", scatter_dimension=0, tiled=True),
        lax.psum_scatter(teach_parts[3], "dp", scatter_dimension=1, tiled=True),
        lax.psum_scatter(teach_parts[4], "dp", scatter_dimension=0, tiled=True),
        lax.psum_scatter(teach_parts[5], "dp", scatter_dimension=0, tiled=True),
        lax.psum_scatter(teach_parts[6], "dp", scatter_dimension=0, tiled=True),
        lax.psum_scatter(teach_parts[7], "dp", scatter_dimension=0, tiled=True),
        lax.psum_scatter(teach_parts[8], "dp", scatter_dimension=0, tiled=True),
        lax.psum_scatter(teach_parts[9], "dp", scatter_dimension=0, tiled=True),
        lax.psum_scatter(learn_parts[0], "dp", scatter_dimension=1, tiled=True),
        lax.psum_scatter(learn_parts[1], "dp", scatter_dimension=1, tiled=True),
        lax.psum_scatter(learn_parts[2], "dp", scatter_dimension=0, tiled=True),
        lax.psum_scatter(learn_parts[3], "dp", scatter_dimension=1, tiled=True),
        lax.psum_scatter(learn_parts[4], "dp", scatter_dimension=0, tiled=True),
        lax.psum_scatter(learn_parts[5], "dp", scatter_dimension=0, tiled=True),
        lax.psum_scatter(learn_parts[6], "dp", scatter_dimension=0, tiled=True),
        lax.psum_scatter(learn_parts[7], "dp", scatter_dimension=0, tiled=True),
        lax.psum_scatter(learn_parts[8], "dp", scatter_dimension=0, tiled=True),
        lax.psum_scatter(learn_parts[9], "dp", scatter_dimension=0, tiled=True),
    )
    totals = lax.psum((teacher[3][0], teacher[3][1], student[3][0], student[3][1]), "dp")
    teacher_matrices = summed[0:10]
    student_matrices = summed[10:20]
    teacher_biases = (totals[0], totals[1])
    student_biases = (totals[2], totals[3])
    return arrange(teacher[0], teacher[1], teacher_matrices, teacher_biases) + arrange(
        student[0], student[1], student_matrices, student_biases
    )


def solution(mesh):
    in_specs = (
        P("dp", "tensor", None),
        P("dp", "tensor", None),
        P("dp"),
        P("dp"),
        P(None, "dp", "tensor"),
        P(None, "tensor"),
        P("tensor", "dp"),
        P("dp"),
        P("dp"),
        P("dp"),
        P("dp", "tensor"),
        P("tensor"),
        P("tensor", "dp"),
        P("dp"),
        P("dp", "tensor", None),
        P("dp", "tensor", None),
        P("dp"),
        P("dp"),
        P(None, "dp", "tensor"),
        P(None, "tensor"),
        P("tensor", "dp"),
        P("dp"),
        P("dp"),
        P("dp"),
        P("dp", "tensor"),
        P("tensor"),
        P("tensor", "dp"),
        P("dp"),
        P("dp"),
        P("tensor"),
    )
    out_specs = (
        P("dp", "tensor", None),
        P("dp", "tensor", None),
        P("dp"),
        P("dp"),
        P(None, "dp", "tensor"),
        P(None, "tensor"),
        P("tensor", "dp"),
        P("dp"),
        P("dp"),
        P("dp"),
        P("dp", "tensor"),
        P("tensor"),
        P("tensor", "dp"),
        P("dp"),
        P("dp", "tensor", None),
        P("dp", "tensor", None),
        P("dp"),
        P("dp"),
        P(None, "dp", "tensor"),
        P(None, "tensor"),
        P("tensor", "dp"),
        P("dp"),
        P("dp"),
        P("dp"),
        P("dp", "tensor"),
        P("tensor"),
        P("tensor", "dp"),
        P("dp"),
    )
    return jax.shard_map(
        on_device, mesh=mesh, in_specs=in_specs, out_specs=out_specs, check_vma=False
    )
```

profile of v0, /device:TPU:0, one launch (start us, length us, event | category | flops | bytes accessed | tf_op | source)
XLA Modules:
  0.0 1425.0 jit_solution(5786993439719821327)
XLA Ops:
  22.5 26.5 %all-reduce.27 = (bf16[1280]{0:T(1024)(128)(2,1)}, bf16[1280]{0:T(1024)(128)(2,1)}, bf16[1280]{0:T(1024)(128)(2,1)S(1)}, bf16[1280]{0:T(1024)(128)(2,1)S(1)}, bf...) all-reduce(bf16[1280]{0:T(1024)(128)(2,1)S(1)} %dynamic-update-slic, ...), channel_id=1, replica_groups=mesh['dp'=8,'tensor'=4] {'dp'}, use_global_device_ids=true, to_apply=%add.4 | all-reduce | flops 12288 | bytes 49152
  56.3 10.9 all_gather.88
  67.2 13.4 all_gather.101
  80.7 9.0 all_gather.102
  108.0 35.6 %all-gather.16.cloned.1.call-done = bf16[1024,1280]{1,0:T(8,128)(2,1)} async-done(((bf16[256,1280]{1,0:T(8,128)(2,1)}), bf16[1024,1280]{1,0:T(8,128)(2,1)}) %all-gather.16.cloned.1.call-update) | async-done | bytes 2621456 | tf_op jit(solution)/shard_map/all_gather | solution.py:102
  143.6 32.2 %all-gather.18.cloned.1.call-done = bf16[3,1280,384]{2,1,0:T(8,128)(2,1)} async-done(((bf16[3,160,384]{2,1,0:T(8,128)(2,1)}), bf16[3,1280,384]{2,1,0:T(8,128)(2,1)}) %all-gather.18.cloned.1.call-update) | async-done | bytes 2949136 | tf_op jit(solution)/shard_map/all_gather | solution.py:148
  175.8 6.0 fusion.47
  184.9 3.0 fusion
  189.5 3.8 fusion.10
  195.8 2.8 fusion.1
  200.5 3.8 fusion.11
  205.2 3.2 convolution_convert_fusion
  209.1 4.2 reduce-scatter.34.cloned.1.call-done
  220.0 46.6 %reduce-scatter.20.cloned.1.call-done = bf16[256,1280]{1,0:T(8,128)(2,1)} async-done(((bf16[1024,1280]{1,0:T(8,128)(2,1)}), bf16[256,1280]{1,0:T(8,128)(2,1)}) %reduce-scatter.20.cloned.1.call-update) | async-done | bytes 655376 | tf_op jit(solution)/shard_map/reduce_scatter | solution.py:110
  273.4 18.7 %all-gather.32.cloned.1.call-done = bf16[768,768]{1,0:T(8,128)(2,1)} async-done(((bf16[96,768]{1,0:T(8,128)(2,1)}), bf16[768,768]{1,0:T(8,128)(2,1)}) %all-gather.32.cloned.1.call-update) | async-done | bytes 1179664 | tf_op jit(solution)/shard_map/all_gather | solution.py:150
  292.1 39.3 %all-gather.30.cloned.1.call-done = bf16[1024,768]{1,0:T(8,128)(2,1)} async-done(((bf16[256,768]{1,0:T(8,128)(2,1)}), bf16[1024,768]{1,0:T(8,128)(2,1)}) %all-gather.30.cloned.1.call-update) | async-done | bytes 1572880 | tf_op jit(solution)/shard_map/all_gather | solution.py:102
  331.4 4.8 fusion.170
  336.2 20.0 %all-gather.34.cloned.1.call-done = bf16[768,768]{0,1:T(8,128)(2,1)} async-done(((bf16[768,96]{0,1:T(8,128)(2,1)}), bf16[768,768]{0,1:T(8,128)(2,1)}) %all-gather.34.cloned.1.call-update) | async-done | bytes 1179664 | tf_op jit(solution)/shard_map/all_gather | solution.py:151
  356.2 38.7 %all-gather.40.cloned.1.call-done = bf16[1,1024,768]{2,1,0:T(8,128)(2,1)} async-done(((bf16[1,256,768]{2,1,0:T(8,128)(2,1)}), bf16[1,1024,768]{2,1,0:T(8,128)(2,1)}) %all-gather.40.cloned.1.call-update) | async-done | bytes 1572880 | tf_op jit(solution)/shard_map/all_gather | solution.py:106
  394.9 6.3 convert_reduce_fusion.4
  405.1 5.5 convolution_convert_fusion.4
  411.0 17.4 %all-gather.22.cloned.1.call-done = bf16[1280,1280]{1,0:T(8,128)(2,1)} async-done(((bf16[160,1280]{1,0:T(8,128)(2,1)}), bf16[1280,1280]{1,0:T(8,128)(2,1)}) %all-gather.22.cloned.1.call-update) | async-done | bytes 3276816 | tf_op jit(solution)/shard_map/all_gather | solution.py:150
  428.4 57.0 %all-gather.20.cloned.1.call-done = bf16[1024,1280]{1,0:T(8,128)(2,1)} async-done(((bf16[256,1280]{1,0:T(8,128)(2,1)}), bf16[1024,1280]{1,0:T(8,128)(2,1)}) %all-gather.20.cloned.1.call-update) | async-done | bytes 2621456 | tf_op jit(solution)/shard_map/all_gather | solution.py:102
  485.4 8.6 fusion.166
  493.9 46.5 %all-gather.38.cloned.1.call-done = bf16[1,1024,1280]{2,1,0:T(8,128)(2,1)} async-done(((bf16[1,256,1280]{2,1,0:T(8,128)(2,1)}), bf16[1,1024,1280]{2,1,0:T(8,128)(2,1)}) %all-gather.38.cloned.1.call-update) | async-done | bytes 2621456 | tf_op jit(solution)/shard_map/all_gather | solution.py:106
  540.4 33.6 %all-gather.24.cloned.1.call-done = bf16[1280,1280]{0,1:T(8,128)(2,1)} async-done(((bf16[1280,160]{0,1:T(8,128)(2,1)}), bf16[1280,1280]{0,1:T(8,128)(2,1)}) %all-gather.24.cloned.1.call-update) | async-done | bytes 3276816 | tf_op jit(solution)/shard_map/all_gather | solution.py:151
  574.0 10.7 convert_reduce_fusion.1
  586.2 4.9 convolution_convert_fusion.1
  591.2 9.7 convolution_convert_fusion.2
  601.0 10.4 reduce-scatter.38.cloned.1.call-done
  613.5 34.4 %reduce-scatter.36.cloned.1.call-done = bf16[256,768]{1,0:T(8,128)(2,1)} async-done(((bf16[1024,768]{1,0:T(8,128)(2,1)}), bf16[256,768]{1,0:T(8,128)(2,1)}) %reduce-scatter.36.cloned.1.call-update) | async-done | bytes 393232 | tf_op jit(solution)/shard_map/reduce_scatter | solution.py:110
  652.7 48.5 %reduce-scatter.24.cloned.1.call-done = bf16[256,1280]{1,0:T(8,128)(2,1)} async-done(((bf16[1024,1280]{1,0:T(8,128)(2,1)}), bf16[256,1280]{1,0:T(8,128)(2,1)}) %reduce-scatter.24.cloned.1.call-update) | async-done | bytes 655376 | tf_op jit(solution)/shard_map/reduce_scatter | solution.py:119
  703.5 51.6 %reduce-scatter.22.cloned.1.call-done = bf16[256,1280]{1,0:T(8,128)(2,1)} async-done(((bf16[1024,1280]{1,0:T(8,128)(2,1)}), bf16[256,1280]{1,0:T(8,128)(2,1)}) %reduce-scatter.22.cloned.1.call-update) | async-done | bytes 655376 | tf_op jit(solution)/shard_map/reduce_scatter | solution.py:110
  755.2 2.8 fusion.156
  760.7 33.2 %all-gather.36.cloned.1.call-done = bf16[1024,768]{1,0:T(8,128)(2,1)} async-done(((bf16[256,768]{1,0:T(8,128)(2,1)}), bf16[1024,768]{1,0:T(8,128)(2,1)}) %all-gather.36.cloned.1.call-update) | async-done | bytes 1572880 | tf_op jit(solution)/shard_map/all_gather | solution.py:106
  799.7 4.3 multiply_reduce_fusion.3
  811.9 5.1 multiply_reduce_fusion.2
  817.1 5.6 multiply_convert_fusion.2
  830.1 4.8 reshape.472
  835.0 3.9 bitcast_convert_fusion.1
  839.2 10.6 all-gather.26.cloned.1.call-done
  849.8 3.0 convolution_convert_fusion.6
  853.0 6.0 fusion.4
  859.0 9.6 multiply_reduce_fusion
  868.6 6.2 multiply_reduce_fusion.1
  878.3 9.7 multiply_convert_fusion.1
  892.7 6.9 multiply_convert_fusion
  903.4 5.0 fusion.95
  911.0 8.4 convolution_bitcast_fusion
  919.3 9.8 copy.70
  929.2 7.8 bitcast_convert_fusion
  937.1 5.2 fusion.63
  942.6 4.7 fusion.172
  947.4 9.8 fusion.38
  957.3 8.9 fusion.168
  977.5 5.3 fusion.152
  987.0 105.4 %all-reduce.30.cloned.1.call-done = f32[3,1280,384]{2,0,1:T(4,128)} async-done(((f32[3,1280,384]{2,0,1:T(4,128)}), f32[3,1280,384]{2,0,1:T(4,128)}) %all-reduce.30.cloned.1.call-update) | async-done | bytes 5898256
  1094.7 52.2 %reduce-scatter.26.cloned.1.call-done = bf16[256,1280]{1,0:T(8,128)(2,1)} async-done(((bf16[1024,1280]{1,0:T(8,128)(2,1)}), bf16[256,1280]{1,0:T(8,128)(2,1)}) %reduce-scatter.26.cloned.1.call-update) | async-done | bytes 655376 | tf_op jit(solution)/shard_map/reduce_scatter | solution.py:119
  1150.3 25.6 %all-reduce.25 = (f32[1280]{0:T(1024)S(1)}, f32[1280]{0:T(1024)S(1)}, f32[2,384]{1,0:T(2,128)}, f32[1280]{0:T(1024)S(1)}, f32[1280]{0:T(1024)S(1)}, /*index=5*/f...) all-reduce(f32[1280]{0:T(1024)S(1)} %get-tuple-element.86, ...), channel_id=8, replica_groups=mesh['dp'=8,'tensor'=4] {'dp'}, use_global_device_ids=true, to_apply=%region_20.21.clone | all-reduce | flops 15488 | bytes 123904
  1178.9 11.3 all-reduce.26
  1193.0 46.7 %reduce-scatter.42.cloned.1.call-done = f32[96,768]{1,0:T(8,128)} async-done(((f32[768,768]{1,0:T(8,128)}), f32[96,768]{1,0:T(8,128)}) %reduce-scatter.42.cloned.1.call-update) | async-done | bytes 294928 | tf_op jit(solution)/shard_map/reduce_scatter | solution.py:361
  1239.6 66.9 %reduce-scatter.32.cloned.1.call-done = f32[1280,160]{0,1:T(8,128)} async-done(((f32[1280,1280]{0,1:T(8,128)}), f32[1280,160]{0,1:T(8,128)}) %reduce-scatter.32.cloned.1.call-update) | async-done | bytes 819216 | tf_op jit(solution)/shard_map/reduce_scatter | solution.py:352
  1306.5 67.4 %reduce-scatter.30.cloned.1.call-done = f32[160,1280]{1,0:T(8,128)} async-done(((f32[1280,1280]{1,0:T(8,128)}), f32[160,1280]{1,0:T(8,128)}) %reduce-scatter.30.cloned.1.call-update) | async-done | bytes 819216 | tf_op jit(solution)/shard_map/reduce_scatter | solution.py:351
  1374.0 44.3 %reduce-scatter.28.cloned.1.call-done = f32[384,160]{0,1:T(8,128)} async-done(((f32[384,1280]{0,1:T(8,128)}), f32[384,160]{0,1:T(8,128)}) %reduce-scatter.28.cloned.1.call-update) | async-done | bytes 245776 | tf_op jit(solution)/shard_map/reduce_scatter | solution.py:350
  (509 shorter events, 141.7 us)
Async XLA Ops:
  7.2 45.2 %copy-start.4 = (bf16[1,256,1280]{2,1,0:T(8,128)(2,1)S(1)}, bf16[1,256,1280]{2,1,0:T(8,128)(2,1)}, u32[]{:S(2)}) copy-start(bf16[1,256,1280]{2,1,0:T(8,128)(2,1)} %param.30) | copy-start | bytes 1966084
  7.2 48.2 %copy-start.118 = (s32[6]{0:T(128)S(1)}, s32[6]{0:T(128)}, u32[]{:S(2)}) copy-start(s32[6]{0:T(128)} %param.59) | copy-start | bytes 76
  7.2 48.7 %copy-start.103 = (bf16[2,192]{1,0:T(2,128)(2,1)S(1)}, bf16[2,192]{1,0:T(2,128)(2,1)}, u32[]{:S(2)}) copy-start(bf16[2,192]{1,0:T(2,128)(2,1)} %param.49) | copy-start | bytes 2308
  7.2 48.7 %copy-start.113 = (bf16[2,384]{1,0:T(2,128)(2,1)S(1)}, bf16[2,384]{1,0:T(2,128)(2,1)}, u32[]{:S(2)}) copy-start(bf16[2,384]{1,0:T(2,128)(2,1)} %param.35) | copy-start | bytes 4612
  7.2 48.8 %copy-start.73 = (bf16[192,96]{1,0:T(8,128)(2,1)S(1)}, bf16[192,96]{1,0:T(8,128)(2,1)}, u32[]{:S(2)}) copy-start(bf16[192,96]{1,0:T(8,128)(2,1)} %param.50) | copy-start | bytes 110596
  7.3 48.9 %copy-start.60 = (bf16[3,96,192]{2,1,0:T(8,128)(2,1)S(1)}, bf16[3,96,192]{2,1,0:T(8,128)(2,1)}, u32[]{:S(2)}) copy-start(bf16[3,96,192]{2,1,0:T(8,128)(2,1)} %param.48) | copy-start | bytes 331780
  7.3 85.9 %all-gather.28.cloned.1.call-start = ((), (), s32[]{:S(2)}) async-start(), calls=%async_computation.28 | async-start | bytes 1966080 | tf_op jit(solution)/shard_map/all_gather | solution.py:102
  9.9 46.3 %copy-start.66 = (bf16[384,160]{0,1:T(8,128)(2,1)S(1)}, bf16[384,160]{0,1:T(8,128)(2,1)}, u32[]{:S(2)}) copy-start(bf16[384,160]{0,1:T(8,128)(2,1)} %param.36) | copy-start | bytes 368644
  11.1 56.1 %copy-start.74 = (f32[256]{0:T(256)}, f32[256]{0:T(256)S(1)}, u32[]{:S(2)}) copy-start(f32[256]{0:T(256)S(1)} %broadcast_multiply_fusion.2) | copy-start | bytes 3076
  51.0 92.6 %all-gather.16.cloned.1.call-start = ((), (), s32[]{:S(2)}) async-start(), calls=%async_computation.15 | async-start | bytes 3276800 | tf_op jit(solution)/shard_map/all_gather | solution.py:102
  52.7 39.3 %copy-start.90 = (f32[256]{0:T(256)}, f32[256]{0:T(256)S(1)}, u32[]{:S(2)}) copy-start(f32[256]{0:T(256)S(1)} %fusion.81) | copy-start | bytes 3076
  53.9 121.9 %all-gather.18.cloned.1.call-start = ((), (), s32[]{:S(2)}) async-start(), calls=%async_computation.16 | async-start | bytes 3317760 | tf_op jit(solution)/shard_map/all_gather | solution.py:148
  54.7 158.6 %reduce-scatter.34.cloned.1.call-start = ((), (), s32[]{:S(2)}) async-start(), calls=%async_computation.29 | async-start | bytes 1966080 | tf_op jit(solution)/shard_map/reduce_scatter | solution.py:110
  90.0 114.4 %copy-start.107 = (f32[384]{0:T(512)}, f32[384]{0:T(512)S(1)}, u32[]{:S(2)}) copy-start(f32[384]{0:T(512)S(1)} %mul.401) | copy-start | bytes 4612
  105.6 76.2 %copy-start.55 = (bf16[3,64,512]{2,1,0:T(8,128)(2,1)}, bf16[3,64,512]{2,1,0:T(8,128)(2,1)S(1)}, u32[]{:S(2)}) copy-start(bf16[3,64,512]{2,1,0:T(8,128)(2,1)S(1)} %fusion.100) | copy-start | bytes 589828
  107.5 159.1 %reduce-scatter.20.cloned.1.call-start = ((), (), s32[]{:S(2)}) async-start(), calls=%async_computation.17 | async-start | bytes 3276800 | tf_op jit(solution)/shard_map/reduce_scatter | solution.py:110
  208.4 83.7 %all-gather.32.cloned.1.call-start = ((), (), s32[]{:S(2)}) async-start(), calls=%async_computation.31 | async-start | bytes 1327104 | tf_op jit(solution)/shard_map/all_gather | solution.py:150
  209.0 122.3 %all-gather.30.cloned.1.call-start = ((), (), s32[]{:S(2)}) async-start(), calls=%async_computation.30 | async-start | bytes 1966080 | tf_op jit(solution)/shard_map/all_gather | solution.py:102
  217.8 138.4 %all-gather.34.cloned.1.call-start = ((), (), s32[]{:S(2)}) async-start(), calls=%async_computation.32 | async-start | bytes 1327104 | tf_op jit(solution)/shard_map/all_gather | solution.py:151
  218.6 176.3 %all-gather.40.cloned.1.call-start = ((), (), s32[]{:S(2)}) async-start(), calls=%async_computation.40 | async-start | bytes 1966080 | tf_op jit(solution)/shard_map/all_gather | solution.py:106
  219.3 209.1 %all-gather.22.cloned.1.call-start = ((), (), s32[]{:S(2)}) async-start(), calls=%async_computation.19 | async-start | bytes 3686400 | tf_op jit(solution)/shard_map/all_gather | solution.py:150
  219.9 265.5 %all-gather.20.cloned.1.call-start = ((), (), s32[]{:S(2)}) async-start(), calls=%async_computation.18 | async-start | bytes 3276800 | tf_op jit(solution)/shard_map/all_gather | solution.py:102
  220.0 53.4 %copy-start.106 = (bf16[768]{0:T(1024)(128)(2,1)S(1)}, bf16[768]{0:T(1024)(128)(2,1)}, u32[]{:S(2)}) copy-start(bf16[768]{0:T(1024)(128)(2,1)} %param.55) | copy-start | bytes 4612
  271.8 268.6 %all-gather.38.cloned.1.call-start = ((), (), s32[]{:S(2)}) async-start(), calls=%async_computation.39 | async-start | bytes 3276800 | tf_op jit(solution)/shard_map/all_gather | solution.py:106
  272.4 301.6 %all-gather.24.cloned.1.call-start = ((), (), s32[]{:S(2)}) async-start(), calls=%async_computation.20 | async-start | bytes 3686400 | tf_op jit(solution)/shard_map/all_gather | solution.py:151
  273.1 338.3 %reduce-scatter.38.cloned.1.call-start = ((), (), s32[]{:S(2)}) async-start(), calls=%async_computation.34 | async-start | bytes 1966080 | tf_op jit(solution)/shard_map/reduce_scatter | solution.py:119
  273.4 131.6 %copy-start.104 = (f32[768]{0:T(1024)}, f32[768]{0:T(1024)S(1)}, u32[]{:S(2)}) copy-start(f32[768]{0:T(1024)S(1)} %convert_element_type.331) | copy-start | bytes 9220
  336.2 66.2 %copy-start.117 = (bf16[768,768]{1,0:T(8,128)(2,1)S(1)}, bf16[768,768]{1,0:T(8,128)(2,1)}, u32[]{:S(2)}) copy-start(bf16[768,768]{1,0:T(8,128)(2,1)} %all-gather.32.cloned.1.call-done) | copy-start | bytes 3538948
  405.0 242.9 %reduce-scatter.36.cloned.1.call-start = ((), (), s32[]{:S(2)}) async-start(), calls=%async_computation.33 | async-start | bytes 1966080 | tf_op jit(solution)/shard_map/reduce_scatter | solution.py:110
  410.5 290.6 %reduce-scatter.24.cloned.1.call-start = ((), (), s32[]{:S(2)}) async-start(), calls=%async_computation.22 | async-start | bytes 3276800 | tf_op jit(solution)/shard_map/reduce_scatter | solution.py:119
  411.0 180.2 %copy-start.95 = (f32[1280]{0:T(1024)}, f32[1280]{0:T(1024)S(1)}, u32[]{:S(2)}) copy-start(f32[1280]{0:T(1024)S(1)} %convert_element_type.289) | copy-start | bytes 15364
  591.1 164.0 %reduce-scatter.22.cloned.1.call-start = ((), (), s32[]{:S(2)}) async-start(), calls=%async_computation.21 | async-start | bytes 3276800 | tf_op jit(solution)/shard_map/reduce_scatter | solution.py:110
  600.9 51.7 %copy-start.99 = (bf16[1280]{0:T(1024)(128)(2,1)S(1)}, bf16[1280]{0:T(1024)(128)(2,1)}, u32[]{:S(2)}) copy-start(bf16[1280]{0:T(1024)(128)(2,1)} %get-tuple-element.129) | copy-start | bytes 7684
  601.0 100.2 %copy-start.11 = (bf16[256,1280]{1,0:T(8,128)(2,1)S(1)}, bf16[256,1280]{1,0:T(8,128)(2,1)}, u32[]{:S(2)}) copy-start(bf16[256,1280]{1,0:T(8,128)(2,1)} %reduce-scatter.20.cloned.1.call-done) | copy-start | bytes 1966084
  601.0 193.0 %all-gather.36.cloned.1.call-start = ((), (), s32[]{:S(2)}) async-start(), calls=%async_computation.35 | async-start | bytes 1966080 | tf_op jit(solution)/shard_map/all_gather | solution.py:106
  650.2 53.3 %copy-start.23 = (f32[256,768]{1,0:T(8,128)}, f32[256,768]{1,0:T(8,128)S(1)}, u32[]{:S(2)}) copy-start(f32[256,768]{1,0:T(8,128)S(1)} %get-tuple-element.137) | copy-start | bytes 2359300
  650.2 107.8 %copy-start.92 = (f32[256]{0:T(256)}, f32[256]{0:T(256)S(1)}, u32[]{:S(2)}) copy-start(f32[256]{0:T(256)S(1)} %negate_multiply_fusion.1) | copy-start | bytes 3076
  652.4 197.4 %all-gather.26.cloned.1.call-start = ((), (), s32[]{:S(2)}) async-start(), calls=%async_computation.23 | async-start | bytes 3276800 | tf_op jit(solution)/shard_map/all_gather | solution.py:106
  760.6 211.8 %reduce-scatter.48.cloned.1.call-start = ((), (), s32[]{:S(2)}) async-start(), calls=%async_computation.42 | async-start | bytes 884736
  760.7 49.1 %copy-start.65 = (f32[3,512]{1,0:T(4,128)}, f32[3,512]{1,0:T(4,128)S(1)}, u32[]{:S(2)}) copy-start(f32[3,512]{1,0:T(4,128)S(1)} %log_add_fusion.2) | copy-start | bytes 18436
  760.7 43.2 %copy-start.63 = (f32[3,512]{1,0:T(4,128)}, f32[3,512]{1,0:T(4,128)S(1)}, u32[]{:S(2)}) copy-start(f32[3,512]{1,0:T(4,128)S(1)} %log_add_fusion.3) | copy-start | bytes 18436
  817.0 157.1 %reduce-scatter.46.cloned.1.call-start = ((), (), s32[]{:S(2)}) async-start(), calls=%async_computation.41 | async-start | bytes 2211840
  834.9 141.0 %reduce-scatter.40.cloned.1.call-start = ((), (), s32[]{:S(2)}) async-start(), calls=%async_computation.36 | async-start | bytes 1966080 | tf_op jit(solution)/shard_map/reduce_scatter | solution.py:119
  838.9 253.5 %all-reduce.30.cloned.1.call-start = ((), (), s32[]{:S(2)}) async-start(), calls=%async_computation.43 | async-start | bytes 15728640
  929.2 217.7 %reduce-scatter.26.cloned.1.call-start = ((), (), s32[]{:S(2)}) async-start(), calls=%async_computation.24 | async-start | bytes 3276800 | tf_op jit(solution)/shard_map/reduce_scatter | solution.py:119
  937.0 255.9 %reduce-scatter.44.cloned.1.call-start = ((), (), s32[]{:S(2)}) async-start(), calls=%async_computation.38 | async-start | bytes 2654208 | tf_op jit(solution)/shard_map/reduce_scatter | solution.py:362
  942.4 297.3 %reduce-scatter.42.cloned.1.call-start = ((), (), s32[]{:S(2)}) async-start(), calls=%async_computation.37 | async-start | bytes 2654208 | tf_op jit(solution)/shard_map/reduce_scatter | solution.py:361
  947.3 359.2 %reduce-scatter.32.cloned.1.call-start = ((), (), s32[]{:S(2)}) async-start(), calls=%async_computation.27 | async-start | bytes 7372800 | tf_op jit(solution)/shard_map/reduce_scatter | solution.py:352
  957.2 416.7 %reduce-scatter.30.cloned.1.call-start = ((), (), s32[]{:S(2)}) async-start(), calls=%async_computation.26 | async-start | bytes 7372800 | tf_op jit(solution)/shard_map/reduce_scatter | solution.py:351
  966.2 452.1 %reduce-scatter.28.cloned.1.call-start = ((), (), s32[]{:S(2)}) async-start(), calls=%async_computation.25 | async-start | bytes 2211840 | tf_op jit(solution)/shard_map/reduce_scatter | solution.py:350
  986.4 160.4 %copy-start.59 = (f32[1280]{0:T(1024)S(1)}, f32[1280]{0:T(1024)}, u32[]{:S(2)}) copy-start(f32[1280]{0:T(1024)} %copy-done.58) | copy-start | bytes 15364
  986.4 160.4 %copy-start.77 = (f32[256]{0:T(256)S(1)}, f32[256]{0:T(256)}, u32[]{:S(2)}) copy-start(f32[256]{0:T(256)} %copy-done.76) | copy-start | bytes 3076
  986.9 161.6 %copy-start.91 = (f32[256]{0:T(256)S(1)}, f32[256]{0:T(256)}, u32[]{:S(2)}) copy-start(f32[256]{0:T(256)} %copy-done.90) | copy-start | bytes 3076
  986.9 161.6 %copy-start.85 = (f32[256]{0:T(256)S(1)}, f32[256]{0:T(256)}, u32[]{:S(2)}) copy-start(f32[256]{0:T(256)} %copy-done.84) | copy-start | bytes 3076
  986.9 163.4 %copy-start.78 = (f32[1280]{0:T(1024)S(1)}, f32[1280]{0:T(1024)}, u32[]{:S(2)}) copy-start(f32[1280]{0:T(1024)} %get-tuple-element.84) | copy-start | bytes 15364
  986.9 163.4 %copy-start.79 = (f32[1280]{0:T(1024)S(1)}, f32[1280]{0:T(1024)}, u32[]{:S(2)}) copy-start(f32[1280]{0:T(1024)} %get-tuple-element.92) | copy-start | bytes 15364
  986.9 163.4 %copy-start.82 = (f32[768]{0:T(1024)S(1)}, f32[768]{0:T(1024)}, u32[]{:S(2)}) copy-start(f32[768]{0:T(1024)} %get-tuple-element.88) | copy-start | bytes 9220
  986.9 163.4 %copy-start.83 = (f32[768]{0:T(1024)S(1)}, f32[768]{0:T(1024)}, u32[]{:S(2)}) copy-start(f32[768]{0:T(1024)} %get-tuple-element.95) | copy-start | bytes 9220
  986.9 163.4 %copy-start.94 = (f32[1280]{0:T(1024)S(1)}, f32[1280]{0:T(1024)}, u32[]{:S(2)}) copy-start(f32[1280]{0:T(1024)} %get-tuple-element.162) | copy-start | bytes 15364
  986.9 163.4 %copy-start.98 = (f32[768]{0:T(1024)S(1)}, f32[768]{0:T(1024)}, u32[]{:S(2)}) copy-start(f32[768]{0:T(1024)} %get-tuple-element.172) | copy-start | bytes 9220
  987.0 203.3 %copy-start.15 = (f32[256,1280]{1,0:T(8,128)S(1)}, f32[256,1280]{1,0:T(8,128)}, u32[]{:S(2)}) copy-start(f32[256,1280]{1,0:T(8,128)} %copy-done.14) | copy-start | bytes 3932164
  987.0 203.3 %copy-start.24 = (bf16[1,256,1280]{2,1,0:T(8,128)(2,1)S(1)}, bf16[1,256,1280]{2,1,0:T(8,128)(2,1)}, u32[]{:S(2)}) copy-start(bf16[1,256,1280]{2,1,0:T(8,128)(2,1)} %param.31) | copy-start | bytes 1966084
  987.0 203.3 %copy-start.87 = (f32[256]{0:T(256)S(1)}, f32[256]{0:T(256)}, u32[]{:S(2)}) copy-start(f32[256]{0:T(256)} %copy-done.86) | copy-start | bytes 3076
  1146.9 43.4 %copy-start.25 = (bf16[256,1280]{1,0:T(8,128)(2,1)S(1)}, bf16[256,1280]{1,0:T(8,128)(2,1)}, u32[]{:S(2)}) copy-start(bf16[256,1280]{1,0:T(8,128)(2,1)} %reduce-scatter.26.cloned.1.call-done) | copy-start | bytes 1966084
  (100 other events, 846.7 us)
Sparse Core Ops, SparseCore 0:
  51.1 36.5 all-gather.27
  89.9 53.6 all-gather.15
  145.5 30.2 all-gather.17
  178.0 35.2 reduce-scatter.33
  215.5 51.0 reduce-scatter.19
  268.3 23.7 all-gather.31
  294.2 37.0 all-gather.29
  333.2 22.9 all-gather.33
  357.8 37.0 all-gather.39
  396.6 31.7 all-gather.21
  430.5 54.7 all-gather.19
  486.8 53.5 all-gather.37
  542.3 31.6 all-gather.23
  576.1 35.2 reduce-scatter.37
  613.6 34.2 reduce-scatter.35
  650.1 51.0 reduce-scatter.23
  703.3 51.7 reduce-scatter.21
  757.2 36.7 all-gather.35
  796.1 53.6 all-gather.25
  852.8 33.8 reduce-scatter.47
  890.2 40.2 reduce-scatter.45
  932.9 35.2 reduce-scatter.39
  971.9 120.4 all-reduce.29
  1094.6 52.2 reduce-scatter.25
  1150.8 42.1 reduce-scatter.43
  1197.1 42.4 reduce-scatter.41
  1243.5 62.9 reduce-scatter.31
  1311.0 62.9 reduce-scatter.29
  1378.0 40.2 reduce-scatter.27
where the time goes:
time: 1430 us
  waiting for transfers between devices  967 us (68%)
  matrix products  200 us (14%)
  blocking collectives  96.7 us (7%)
  other arithmetic  80.5 us (6%)
  local copies, waits for them, and re-layouts  57.9 us (4%)
  between operations  19.8 us (1%)
    reduce_scatter x4, waiting for transfers between devices, sum_rows(): lax.psum_scatter(jnp.dot(left_rows, right_weight, preferred_element_type=...  137 us
    all_gather x4, waiting for transfers between devices, gather_rows(): return lax.all_gather(normed, 'tensor', axis=0, tiled=True)  132 us
    all_gather x4, waiting for transfers between devices, gather_grads(): return lax.all_gather(branch_grad, 'tensor', axis=0, tiled=True)  129 us
    reduce_scatter x4, waiting for transfers between devices, back_rows(): lax.psum_scatter(jnp.einsum('sle,sde->ld', grad_stack, weight_stack, pref...  111 us
    unnamed x32, waiting for transfers between devices  110 us
    reduce_scatter x1, waiting for transfers between devices, on_device(): lax.psum_scatter(teach_parts[2], 'dp', scatter_dimension=0, tiled=True)  67.4 us
    reduce_scatter x1, waiting for transfers between devices, on_device(): lax.psum_scatter(teach_parts[3], 'dp', scatter_dimension=1, tiled=True)  66.9 us
    all_gather x2, waiting for transfers between devices, run_block(): lax.all_gather(proj_weight, 'dp', axis=1, tiled=True)  53.6 us
  transfers between devices with their start and end apart: 29, of which 25 were waited for; matrix products, arithmetic and copies ran while one was open for 22% of the time, Pallas kernels for 0%

commit v1 on v0

--- a/solution.py
+++ b/solution.py
@@ -7,6 +7,18 @@
 SPAN = 256
 epsilon = 1e-05
 negative = -1e30
+
+
+def collect(value, axis, dim):
+    ways, here = (lax.axis_size(axis), lax.axis_index(axis))
+    grown, reach = (value, 1)
+    while reach < ways:
+        theirs = lax.ppermute(grown, axis, [(d, d ^ reach) for d in range(ways)])
+        mine_first = jnp.concatenate([grown, theirs], axis=dim)
+        theirs_first = jnp.concatenate([theirs, grown], axis=dim)
+        grown = jnp.where(here & reach == 0, mine_first, theirs_first)
+        reach = 2 * reach
+    return grown
 
 
 def layer_norm(values, norm_gain, norm_shift):
@@ -103,7 +115,7 @@
 
 
 def gather_grads(branch_grad):
-    return lax.all_gather(branch_grad, "tensor", axis=0, tiled=True)
+    return collect(branch_grad, "tensor", 0)
 
 
 def sum_rows(left_rows, right_weight):

time: 1430 us -> 1360 us (0.951)
  waiting for transfers between devices: 967 us -> 872 us
    ppermute x0 -> x8, waiting for transfers between devices: none -> 177 us  [collect(): theirs = lax.ppermute(grown, axis, [(d, d ^ reach) for d in range(ways)])]
    all_gather x4 -> x0, waiting for transfers between devices: 129 us -> none  [gather_grads(): return lax.all_gather(branch_grad, 'tensor', axis=0, tiled=True)]
    unnamed x32 -> x28, waiting for transfers between devices: 110 us -> 52.8 us
    reduce_scatter x4, waiting for transfers between devices: 137 us -> 86.2 us  [sum_rows(): lax.psum_scatter(jnp.dot(left_rows, right_weight, preferred_element_type=...]
    all_gather x4, waiting for transfers between devices: 132 us -> 175 us  [gather_rows(): return lax.all_gather(normed, 'tensor', axis=0, tiled=True)]
    reduce_scatter x4, waiting for transfers between devices: 111 us -> 70.3 us  [back_rows(): lax.psum_scatter(jnp.einsum('sle,sde->ld', grad_stack, weight_stack, pref...]
    all_gather x2, waiting for transfers between devices: 36 us -> 6.86 us  [run_block(): lax.all_gather(fc_weight, 'dp', axis=0, tiled=True)]
    unnamed x316 -> x298, local copies, waits for them, and re-layouts: 42 us -> 44.3 us
  transfers between devices with their start and end apart: 29 -> 33, of which waited for: 25 -> 24; matrix products, arithmetic and copies ran while one was open for 22% -> 24% of each run, Pallas kernels for 0% -> 0%
where the time goes in v1:
time: 1360 us; the launch traced here: 1350 us
  waiting for transfers between devices  872 us (64%)
  matrix products  203 us (15%)
  blocking collectives  96.7 us (7%)
  other arithmetic  89.2 us (7%)
  local copies, waits for them, and re-layouts  60.4 us (4%)
  between operations  19.4 us (1%)
    ppermute x8, waiting for transfers between devices, collect(): theirs = lax.ppermute(grown, axis, [(d, d ^ reach) for d in range(ways)])  177 us
    all_gather x4, waiting for transfers between devices, gather_rows(): return lax.all_gather(normed, 'tensor', axis=0, tiled=True)  175 us
    reduce_scatter x4, waiting for transfers between devices, sum_rows(): lax.psum_scatter(jnp.dot(left_rows, right_weight, preferred_element_type=...  86.2 us
    reduce_scatter x4, waiting for transfers between devices, back_rows(): lax.psum_scatter(jnp.einsum('sle,sde->ld', grad_stack, weight_stack, pref...  70.3 us
    reduce_scatter x1, waiting for transfers between devices, on_device(): lax.psum_scatter(teach_parts[2], 'dp', scatter_dimension=0, tiled=True)  67.3 us
    reduce_scatter x1, waiting for transfers between devices, on_device(): lax.psum_scatter(teach_parts[3], 'dp', scatter_dimension=1, tiled=True)  67.1 us
    unnamed x28, waiting for transfers between devices  52.8 us
    unnamed x2, blocking collectives  52 us
  transfers between devices with their start and end apart: 33, of which 24 were waited for; matrix products, arithmetic and copies ran while one was open for 24% of the time, Pallas kernels for 0%

profile of v1, /device:TPU:0, one launch (start us, length us, event | category | flops | bytes accessed | tf_op | source)
XLA Modules:
  0.0 1352.5 jit_solution(13634727479654542177)
XLA Ops:
  23.1 26.5 %all-reduce.27 = (bf16[1280]{0:T(1024)(128)(2,1)S(1)}, bf16[1280]{0:T(1024)(128)(2,1)S(1)}, bf16[1280]{0:T(1024)(128)(2,1)S(1)}, bf16[1280]{0:T(1024)(128)(2,1)S...) all-reduce(bf16[1280]{0:T(1024)(128)(2,1)S(1)} %dynamic-update-slic, ...), channel_id=1, replica_groups=mesh['dp'=8,'tensor'=4] {'dp'}, use_global_device_ids=true, to_apply=%add.4 | all-reduce | flops 12288 | bytes 49152
  58.5 10.9 all_gather.76
  69.5 13.4 all_gather.87
  82.9 9.0 all_gather.88
  109.6 35.0 %all-gather.10.cloned.1.call-done = bf16[1024,1280]{1,0:T(8,128)(2,1)} async-done(((bf16[256,1280]{1,0:T(8,128)(2,1)}), bf16[1024,1280]{1,0:T(8,128)(2,1)}) %all-gather.10.cloned.1.call-update) | async-done | bytes 2621456 | tf_op jit(solution)/shard_map/all_gather | solution.py:114
  144.7 32.2 %all-gather.12.cloned.1.call-done = bf16[3,1280,384]{2,1,0:T(8,128)(2,1)} async-done(((bf16[3,160,384]{2,1,0:T(8,128)(2,1)}), bf16[3,1280,384]{2,1,0:T(8,128)(2,1)}) %all-gather.12.cloned.1.call-update) | async-done | bytes 2949136 | tf_op jit(solution)/shard_map/all_gather | solution.py:160
  176.9 6.0 fusion.41
  186.0 3.0 fusion
  190.5 3.8 fusion.10
  196.8 2.8 fusion.1
  201.3 3.8 fusion.11
  206.1 3.1 convolution_convert_fusion
  209.9 4.4 reduce-scatter.34.cloned.1.call-done
  220.4 47.2 %reduce-scatter.20.cloned.1.call-done = bf16[256,1280]{1,0:T(8,128)(2,1)} async-done(((bf16[1024,1280]{1,0:T(8,128)(2,1)}), bf16[256,1280]{1,0:T(8,128)(2,1)}) %reduce-scatter.20.cloned.1.call-update) | async-done | bytes 655376 | tf_op jit(solution)/shard_map/reduce_scatter | solution.py:122
  273.5 10.0 collective-permute-done.4
  286.3 6.8 all-gather.24.cloned.1.call-done
  293.1 52.3 %all-gather.22.cloned.1.call-done = bf16[1024,768]{1,0:T(8,128)(2,1)} async-done(((bf16[256,768]{1,0:T(8,128)(2,1)}), bf16[1024,768]{1,0:T(8,128)(2,1)}) %all-gather.22.cloned.1.call-update) | async-done | bytes 1572880 | tf_op jit(solution)/shard_map/all_gather | solution.py:114
  345.4 4.8 fusion.162
  350.2 20.0 %all-gather.26.cloned.1.call-done = bf16[768,768]{0,1:T(8,128)(2,1)} async-done(((bf16[768,96]{0,1:T(8,128)(2,1)}), bf16[768,768]{0,1:T(8,128)(2,1)}) %all-gather.26.cloned.1.call-update) | async-done | bytes 1179664 | tf_op jit(solution)/shard_map/all_gather | solution.py:163
  370.3 6.6 convert_reduce_fusion.4
  382.2 15.4 %collective-permute-done = bf16[256,1280]{1,0:T(8,128)(2,1)S(1)} collective-permute-done((bf16[256,1280]{1,0:T(8,128)(2,1)S(1)}, bf16[256,1280]{1,0:T(8,128)(2,1)S(1)}, u32[]{:S(2)}, u32[]{:S(2)}) %collective-permute-start) | collective-permute-done | bytes 655392 | tf_op jit(solution)/shard_map/ppermute | solution.py:16
  401.7 5.5 convolution_convert_fusion.4
  407.5 87.8 %all-gather.14.cloned.1.call-done = bf16[1024,1280]{1,0:T(8,128)(2,1)} async-done(((bf16[256,1280]{1,0:T(8,128)(2,1)}), bf16[1024,1280]{1,0:T(8,128)(2,1)}) %all-gather.14.cloned.1.call-update) | async-done | bytes 2621456 | tf_op jit(solution)/shard_map/all_gather | solution.py:114
  495.3 8.6 fusion.158
  503.9 25.2 %all-gather.18.cloned.1.call-done = bf16[1280,1280]{0,1:T(8,128)(2,1)} async-done(((bf16[1280,160]{0,1:T(8,128)(2,1)}), bf16[1280,1280]{0,1:T(8,128)(2,1)}) %all-gather.18.cloned.1.call-update) | async-done | bytes 3276816 | tf_op jit(solution)/shard_map/all_gather | solution.py:163
  529.1 12.3 convert_reduce_fusion.1
  542.9 4.9 convolution_convert_fusion.1
  548.4 18.2 %reduce-scatter.38.cloned.1.call-done = bf16[256,768]{1,0:T(8,128)(2,1)} async-done(((bf16[1024,768]{1,0:T(8,128)(2,1)}), bf16[256,768]{1,0:T(8,128)(2,1)}) %reduce-scatter.38.cloned.1.call-update) | async-done | bytes 393232 | tf_op jit(solution)/shard_map/reduce_scatter | solution.py:131
  568.6 34.6 %reduce-scatter.36.cloned.1.call-done = bf16[256,768]{1,0:T(8,128)(2,1)} async-done(((bf16[1024,768]{1,0:T(8,128)(2,1)}), bf16[256,768]{1,0:T(8,128)(2,1)}) %reduce-scatter.36.cloned.1.call-update) | async-done | bytes 393232 | tf_op jit(solution)/shard_map/reduce_scatter | solution.py:122
  605.5 9.9 convolution_convert_fusion.2
  616.1 27.3 %collective-permute-done.6 = bf16[256,768]{1,0:T(8,128)(2,1)S(1)} collective-permute-done((bf16[256,768]{1,0:T(8,128)(2,1)S(1)}, bf16[256,768]{1,0:T(8,128)(2,1)S(1)}, u32[]{:S(2)}, u32[]{:S(2)}) %collective-permute-start.6) | collective-permute-done | bytes 393248 | tf_op jit(solution)/shard_map/ppermute | solution.py:16
  643.9 52.3 %collective-permute-done.7 = bf16[512,768]{1,0:T(8,128)(2,1)S(1)} collective-permute-done((bf16[512,768]{1,0:T(8,128)(2,1)S(1)}, bf16[512,768]{1,0:T(8,128)(2,1)S(1)}, u32[]{:S(2)}, u32[]{:S(2)}) %collective-permute-start.7) | collective-permute-done | bytes 786464 | tf_op jit(solution)/shard_map/ppermute | solution.py:16
  697.1 2.9 convolution_bitcast_fusion.1
  712.0 3.6 multiply_reduce_fusion.2
  715.9 5.5 multiply_convert_fusion.2
  729.6 4.6 reshape.468
  736.7 2.8 fusion.148
  740.3 16.2 %collective-permute-done.2 = bf16[256,1280]{1,0:T(8,128)(2,1)S(1)} collective-permute-done((bf16[256,1280]{1,0:T(8,128)(2,1)S(1)}, bf16[256,1280]{1,0:T(8,128)(2,1)S(1)}, u32[]{:S(2)}, u32[]{:S(2)}) %collective-permute-start.2) | collective-permute-done | bytes 655392 | tf_op jit(solution)/shard_map/ppermute | solution.py:16
  761.7 55.5 %collective-permute-done.3 = bf16[512,1280]{1,0:T(8,128)(2,1)} collective-permute-done((bf16[512,1280]{1,0:T(8,128)(2,1)}, bf16[512,1280]{1,0:T(8,128)(2,1)}, u32[]{:S(2)}, u32[]{:S(2)}) %collective-permute-start.3) | collective-permute-done | bytes 1310752 | tf_op jit(solution)/shard_map/ppermute | solution.py:16
  817.3 4.3 convolution_convert_fusion.6
  821.8 6.2 fusion.4
  828.0 9.3 multiply_reduce_fusion
  837.4 6.2 multiply_reduce_fusion.1
  847.1 9.8 multiply_convert_fusion.1
  861.5 6.7 multiply_convert_fusion
  873.4 5.0 fusion.83
  881.7 8.3 convolution_bitcast_fusion
  890.1 9.8 copy.70
  899.9 7.7 bitcast_convert_fusion
  907.9 5.8 fusion.143
  913.8 4.7 fusion.164
  918.6 11.0 fusion.145
  929.7 9.0 fusion.160
  942.9 4.2 convert_reduce_fusion
  956.0 6.3 fusion.140
  967.1 3.2 convert_reduce_fusion.2
  970.5 49.2 %all-reduce.30.cloned.1.call-done = f32[3,1280,384]{2,0,1:T(4,128)} async-done(((f32[3,1280,384]{2,0,1:T(4,128)}), f32[3,1280,384]{2,0,1:T(4,128)}) %all-reduce.30.cloned.1.call-update) | async-done | bytes 5898256
  1022.0 52.1 %reduce-scatter.26.cloned.1.call-done = bf16[256,1280]{1,0:T(8,128)(2,1)} async-done(((bf16[1024,1280]{1,0:T(8,128)(2,1)}), bf16[256,1280]{1,0:T(8,128)(2,1)}) %reduce-scatter.26.cloned.1.call-update) | async-done | bytes 655376 | tf_op jit(solution)/shard_map/reduce_scatter | solution.py:131
  1077.7 25.6 %all-reduce.25 = (f32[1280]{0:T(1024)S(1)}, f32[1280]{0:T(1024)S(1)}, f32[2,384]{1,0:T(2,128)}, f32[1280]{0:T(1024)S(1)}, f32[1280]{0:T(1024)S(1)}, /*index=5*/f...) all-reduce(f32[1280]{0:T(1024)S(1)} %get-tuple-element.86, ...), channel_id=6, replica_groups=mesh['dp'=8,'tensor'=4] {'dp'}, use_global_device_ids=true, to_apply=%region_20.21.clone | all-reduce | flops 15488 | bytes 123904
  1106.3 11.3 all-reduce.26
  1120.3 46.8 %reduce-scatter.42.cloned.1.call-done = f32[96,768]{1,0:T(8,128)} async-done(((f32[768,768]{1,0:T(8,128)}), f32[96,768]{1,0:T(8,128)}) %reduce-scatter.42.cloned.1.call-update) | async-done | bytes 294928 | tf_op jit(solution)/shard_map/reduce_scatter | solution.py:373
  1167.1 67.1 %reduce-scatter.32.cloned.1.call-done = f32[1280,160]{0,1:T(8,128)} async-done(((f32[1280,1280]{0,1:T(8,128)}), f32[1280,160]{0,1:T(8,128)}) %reduce-scatter.32.cloned.1.call-update) | async-done | bytes 819216 | tf_op jit(solution)/shard_map/reduce_scatter | solution.py:364
  1234.2 67.3 %reduce-scatter.30.cloned.1.call-done = f32[160,1280]{1,0:T(8,128)} async-done(((f32[1280,1280]{1,0:T(8,128)}), f32[160,1280]{1,0:T(8,128)}) %reduce-scatter.30.cloned.1.call-update) | async-done | bytes 819216 | tf_op jit(solution)/shard_map/reduce_scatter | solution.py:363
  1301.5 44.3 %reduce-scatter.28.cloned.1.call-done = f32[384,160]{0,1:T(8,128)} async-done(((f32[384,1280]{0,1:T(8,128)}), f32[384,160]{0,1:T(8,128)}) %reduce-scatter.28.cloned.1.call-update) | async-done | bytes 245776 | tf_op jit(solution)/shard_map/reduce_scatter | solution.py:362
  (499 shorter events, 156.8 us)
Async XLA Ops:
  7.2 46.3 %copy-start.4 = (bf16[1,256,1280]{2,1,0:T(8,128)(2,1)S(1)}, bf16[1,256,1280]{2,1,0:T(8,128)(2,1)}, u32[]{:S(2)}) copy-start(bf16[1,256,1280]{2,1,0:T(8,128)(2,1)} %param.30) | copy-start | bytes 1966084
  7.2 50.4 %copy-start.109 = (s32[6]{0:T(128)S(1)}, s32[6]{0:T(128)}, u32[]{:S(2)}) copy-start(s32[6]{0:T(128)} %param.59) | copy-start | bytes 76
  7.2 51.0 %copy-start.96 = (bf16[2,192]{1,0:T(2,128)(2,1)S(1)}, bf16[2,192]{1,0:T(2,128)(2,1)}, u32[]{:S(2)}) copy-start(bf16[2,192]{1,0:T(2,128)(2,1)} %param.49) | copy-start | bytes 2308
  7.2 51.0 %copy-start.104 = (bf16[2,384]{1,0:T(2,128)(2,1)S(1)}, bf16[2,384]{1,0:T(2,128)(2,1)}, u32[]{:S(2)}) copy-start(bf16[2,384]{1,0:T(2,128)(2,1)} %param.35) | copy-start | bytes 4612
  7.2 51.0 %copy-start.69 = (bf16[192,96]{1,0:T(8,128)(2,1)S(1)}, bf16[192,96]{1,0:T(8,128)(2,1)}, u32[]{:S(2)}) copy-start(bf16[192,96]{1,0:T(8,128)(2,1)} %param.50) | copy-start | bytes 110596
  7.3 87.0 %all-gather.20.cloned.1.call-start = ((), (), s32[]{:S(2)}) async-start(), calls=%async_computation.27 | async-start | bytes 1966080 | tf_op jit(solution)/shard_map/all_gather | solution.py:114
  9.9 48.4 %copy-start.65 = (bf16[3,96,192]{2,1,0:T(8,128)(2,1)S(1)}, bf16[3,96,192]{2,1,0:T(8,128)(2,1)}, u32[]{:S(2)}) copy-start(bf16[3,96,192]{2,1,0:T(8,128)(2,1)} %param.48) | copy-start | bytes 331780
  11.1 47.4 %copy-start.66 = (bf16[384,160]{0,1:T(8,128)(2,1)S(1)}, bf16[384,160]{0,1:T(8,128)(2,1)}, u32[]{:S(2)}) copy-start(bf16[384,160]{0,1:T(8,128)(2,1)} %param.36) | copy-start | bytes 368644
  11.1 47.4 %copy-start.70 = (f32[256]{0:T(256)}, f32[256]{0:T(256)S(1)}, u32[]{:S(2)}) copy-start(f32[256]{0:T(256)S(1)} %broadcast_multiply_fusion.2) | copy-start | bytes 3076
  52.2 92.5 %all-gather.10.cloned.1.call-start = ((), (), s32[]{:S(2)}) async-start(), calls=%async_computation.15 | async-start | bytes 3276800 | tf_op jit(solution)/shard_map/all_gather | solution.py:114
  56.2 120.7 %all-gather.12.cloned.1.call-start = ((), (), s32[]{:S(2)}) async-start(), calls=%async_computation.16 | async-start | bytes 3317760 | tf_op jit(solution)/shard_map/all_gather | solution.py:160
  56.9 157.4 %reduce-scatter.34.cloned.1.call-start = ((), (), s32[]{:S(2)}) async-start(), calls=%async_computation.28 | async-start | bytes 1966080 | tf_op jit(solution)/shard_map/reduce_scatter | solution.py:122
  92.2 113.0 %copy-start.99 = (f32[384]{0:T(512)}, f32[384]{0:T(512)S(1)}, u32[]{:S(2)}) copy-start(f32[384]{0:T(512)S(1)} %mul.401) | copy-start | bytes 4612
  109.0 158.6 %reduce-scatter.20.cloned.1.call-start = ((), (), s32[]{:S(2)}) async-start(), calls=%async_computation.17 | async-start | bytes 3276800 | tf_op jit(solution)/shard_map/reduce_scatter | solution.py:122
  209.3 83.9 %all-gather.24.cloned.1.call-start = ((), (), s32[]{:S(2)}) async-start(), calls=%async_computation.30 | async-start | bytes 1327104 | tf_op jit(solution)/shard_map/all_gather | solution.py:162
  209.8 135.6 %all-gather.22.cloned.1.call-start = ((), (), s32[]{:S(2)}) async-start(), calls=%async_computation.29 | async-start | bytes 1966080 | tf_op jit(solution)/shard_map/all_gather | solution.py:114
  218.8 151.4 %all-gather.26.cloned.1.call-start = ((), (), s32[]{:S(2)}) async-start(), calls=%async_computation.31 | async-start | bytes 1327104 | tf_op jit(solution)/shard_map/all_gather | solution.py:163
  219.6 187.9 %all-gather.16.cloned.1.call-start = ((), (), s32[]{:S(2)}) async-start(), calls=%async_computation.19 | async-start | bytes 3686400 | tf_op jit(solution)/shard_map/all_gather | solution.py:162
  220.3 52.5 %copy-start.34 = (bf16[1,256,768]{2,1,0:T(8,128)(2,1)S(1)}, bf16[1,256,768]{2,1,0:T(8,128)(2,1)}, u32[]{:S(2)}) copy-start(bf16[1,256,768]{2,1,0:T(8,128)(2,1)} %param.45) | copy-start | bytes 1179652
  220.3 275.0 %all-gather.14.cloned.1.call-start = ((), (), s32[]{:S(2)}) async-start(), calls=%async_computation.18 | async-start | bytes 3276800 | tf_op jit(solution)/shard_map/all_gather | solution.py:114
  271.8 257.3 %all-gather.18.cloned.1.call-start = ((), (), s32[]{:S(2)}) async-start(), calls=%async_computation.20 | async-start | bytes 3686400 | tf_op jit(solution)/shard_map/all_gather | solution.py:163
  272.6 294.0 %reduce-scatter.38.cloned.1.call-start = ((), (), s32[]{:S(2)}) async-start(), calls=%async_computation.33 | async-start | bytes 1966080 | tf_op jit(solution)/shard_map/reduce_scatter | solution.py:131
  272.8 10.8 collective-permute-start.4
  283.9 86.4 %copy-start.35 = (bf16[512,768]{1,0:T(8,128)(2,1)}, bf16[512,768]{1,0:T(8,128)(2,1)S(1)}, u32[]{:S(2)}) copy-start(bf16[512,768]{1,0:T(8,128)(2,1)S(1)} %maximum_select_fusion.6) | copy-start | bytes 2359300
  283.9 66.3 %collective-permute-start.5 = (bf16[512,768]{1,0:T(8,128)(2,1)S(1)}, bf16[512,768]{1,0:T(8,128)(2,1)}, u32[]{:S(2)}, u32[]{:S(2)}) collective-permute-start(bf16[512,768]{1,0:T(8,128)(2,1)S(1)} %maximum_select_fusion.6), channel_id=1, source_target_pairs={{0,2},{1,3},{2,0},{3,1},{4,6},{5,7},{6,4},{7,5},{8,10},{9,11},{10,... | collective-permute-start | bytes 2359304 | tf_op jit(solution)/shard_map/ppermute | solution.py:16
  286.3 115.4 %copy-start.97 = (f32[768]{0:T(1024)}, f32[768]{0:T(1024)S(1)}, u32[]{:S(2)}) copy-start(f32[768]{0:T(1024)S(1)} %convert_element_type.331) | copy-start | bytes 9220
  380.6 222.6 %reduce-scatter.36.cloned.1.call-start = ((), (), s32[]{:S(2)}) async-start(), calls=%async_computation.32 | async-start | bytes 1966080 | tf_op jit(solution)/shard_map/reduce_scatter | solution.py:122
  380.6 17.0 %collective-permute-start = (bf16[256,1280]{1,0:T(8,128)(2,1)S(1)}, bf16[256,1280]{1,0:T(8,128)(2,1)S(1)}, u32[]{:S(2)}, u32[]{:S(2)}) collective-permute-start(bf16[256,1280]{1,0:T(8,128)(2,1)S(1)} %bitcast.310), channel_id=1, source_target_pairs={{0,1},{1,0},{2,3},{3,2},{4,5},{5,4},{6,7},{7,6},{8,9},{9,8},{10,11... | collective-permute-start | bytes 1966088 | tf_op jit(solution)/shard_map/ppermute | solution.py:16
  399.2 104.7 %collective-permute-start.1 = (bf16[512,1280]{1,0:T(8,128)(2,1)}, bf16[512,1280]{1,0:T(8,128)(2,1)}, u32[]{:S(2)}, u32[]{:S(2)}) collective-permute-start(bf16[512,1280]{1,0:T(8,128)(2,1)} %maximum_select_fusion.4), channel_id=1, source_target_pairs={{0,2},{1,3},{2,0},{3,1},{4,6},{5,7},{6,4},{7,5},{8,10},{9,11},{10,... | collective-permute-start | bytes 3932168 | tf_op jit(solution)/shard_map/ppermute | solution.py:16
  407.2 327.1 %reduce-scatter.24.cloned.1.call-start = ((), (), s32[]{:S(2)}) async-start(), calls=%async_computation.22 | async-start | bytes 3276800 | tf_op jit(solution)/shard_map/reduce_scatter | solution.py:131
  547.9 188.9 %reduce-scatter.22.cloned.1.call-start = ((), (), s32[]{:S(2)}) async-start(), calls=%async_computation.21 | async-start | bytes 3276800 | tf_op jit(solution)/shard_map/reduce_scatter | solution.py:122
  615.4 333.9 %reduce-scatter.48.cloned.1.call-start = ((), (), s32[]{:S(2)}) async-start(), calls=%async_computation.38 | async-start | bytes 884736
  615.7 27.7 %collective-permute-start.6 = (bf16[256,768]{1,0:T(8,128)(2,1)S(1)}, bf16[256,768]{1,0:T(8,128)(2,1)S(1)}, u32[]{:S(2)}, u32[]{:S(2)}) collective-permute-start(bf16[256,768]{1,0:T(8,128)(2,1)S(1)} %fusion.119), channel_id=1, source_target_pairs={{0,1},{1,0},{2,3},{3,2},{4,5},{5,4},{6,7},{7,6},{8,9},{9,8},{10,11... | collective-permute-start | bytes 1179656 | tf_op jit(solution)/shard_map/ppermute | solution.py:16
  643.8 52.5 %copy-start.37 = (bf16[512,768]{1,0:T(8,128)(2,1)}, bf16[512,768]{1,0:T(8,128)(2,1)S(1)}, u32[]{:S(2)}) copy-start(bf16[512,768]{1,0:T(8,128)(2,1)S(1)} %maximum_select_fusion.7) | copy-start | bytes 2359300
  643.8 52.4 %collective-permute-start.7 = (bf16[512,768]{1,0:T(8,128)(2,1)S(1)}, bf16[512,768]{1,0:T(8,128)(2,1)S(1)}, u32[]{:S(2)}, u32[]{:S(2)}) collective-permute-start(bf16[512,768]{1,0:T(8,128)(2,1)S(1)} %maximum_select_fusion.7), channel_id=1, source_target_pairs={{0,2},{1,3},{2,0},{3,1},{4,6},{5,7},{6,4},{7,5},{8,10},{9,11},{10,... | collective-permute-start | bytes 2359304 | tf_op jit(solution)/shard_map/ppermute | solution.py:16
  715.6 235.3 %reduce-scatter.46.cloned.1.call-start = ((), (), s32[]{:S(2)}) async-start(), calls=%async_computation.37 | async-start | bytes 2211840
  734.3 218.6 %reduce-scatter.40.cloned.1.call-start = ((), (), s32[]{:S(2)}) async-start(), calls=%async_computation.34 | async-start | bytes 1966080 | tf_op jit(solution)/shard_map/reduce_scatter | solution.py:131
  739.8 16.7 %collective-permute-start.2 = (bf16[256,1280]{1,0:T(8,128)(2,1)S(1)}, bf16[256,1280]{1,0:T(8,128)(2,1)S(1)}, u32[]{:S(2)}, u32[]{:S(2)}) collective-permute-start(bf16[256,1280]{1,0:T(8,128)(2,1)S(1)} %fusion.104), channel_id=1, source_target_pairs={{0,1},{1,0},{2,3},{3,2},{4,5},{5,4},{6,7},{7,6},{8,9},{9,8},{10,11... | collective-permute-start | bytes 1966088 | tf_op jit(solution)/shard_map/ppermute | solution.py:16
  758.2 59.1 %collective-permute-start.3 = (bf16[512,1280]{1,0:T(8,128)(2,1)}, bf16[512,1280]{1,0:T(8,128)(2,1)}, u32[]{:S(2)}, u32[]{:S(2)}) collective-permute-start(bf16[512,1280]{1,0:T(8,128)(2,1)} %maximum_select_fusion.5), channel_id=1, source_target_pairs={{0,2},{1,3},{2,0},{3,1},{4,6},{5,7},{6,4},{7,5},{8,10},{9,11},{10,... | collective-permute-start | bytes 3932168 | tf_op jit(solution)/shard_map/ppermute | solution.py:16
  761.5 60.1 %copy-start.105 = (bf16[6]{0:T(256)(128)(2,1)S(1)}, bf16[6]{0:T(256)(128)(2,1)}, u32[]{:S(2)}) copy-start(bf16[6]{0:T(256)(128)(2,1)} %get-tuple-element.152) | copy-start | bytes 40
  761.5 258.2 %all-reduce.30.cloned.1.call-start = ((), (), s32[]{:S(2)}) async-start(), calls=%async_computation.39 | async-start | bytes 15728640
  899.9 174.3 %reduce-scatter.26.cloned.1.call-start = ((), (), s32[]{:S(2)}) async-start(), calls=%async_computation.23 | async-start | bytes 3276800 | tf_op jit(solution)/shard_map/reduce_scatter | solution.py:131
  907.7 212.6 %reduce-scatter.44.cloned.1.call-start = ((), (), s32[]{:S(2)}) async-start(), calls=%async_computation.36 | async-start | bytes 2654208 | tf_op jit(solution)/shard_map/reduce_scatter | solution.py:374
  913.8 253.4 %reduce-scatter.42.cloned.1.call-start = ((), (), s32[]{:S(2)}) async-start(), calls=%async_computation.35 | async-start | bytes 2654208 | tf_op jit(solution)/shard_map/reduce_scatter | solution.py:373
  918.5 315.6 %reduce-scatter.32.cloned.1.call-start = ((), (), s32[]{:S(2)}) async-start(), calls=%async_computation.26 | async-start | bytes 7372800 | tf_op jit(solution)/shard_map/reduce_scatter | solution.py:364
  929.6 371.8 %reduce-scatter.30.cloned.1.call-start = ((), (), s32[]{:S(2)}) async-start(), calls=%async_computation.25 | async-start | bytes 7372800 | tf_op jit(solution)/shard_map/reduce_scatter | solution.py:363
  938.7 407.0 %reduce-scatter.28.cloned.1.call-start = ((), (), s32[]{:S(2)}) async-start(), calls=%async_computation.24 | async-start | bytes 2211840 | tf_op jit(solution)/shard_map/reduce_scatter | solution.py:362
  967.1 107.0 %copy-start.62 = (f32[1280]{0:T(1024)S(1)}, f32[1280]{0:T(1024)}, u32[]{:S(2)}) copy-start(f32[1280]{0:T(1024)} %copy-done.61) | copy-start | bytes 15364
  967.1 107.0 %copy-start.73 = (f32[256]{0:T(256)S(1)}, f32[256]{0:T(256)}, u32[]{:S(2)}) copy-start(f32[256]{0:T(256)} %copy-done.72) | copy-start | bytes 3076
  970.4 105.4 %copy-start.89 = (f32[256]{0:T(256)S(1)}, f32[256]{0:T(256)}, u32[]{:S(2)}) copy-start(f32[256]{0:T(256)} %copy-done.88) | copy-start | bytes 3076
  970.4 105.4 %copy-start.84 = (f32[256]{0:T(256)S(1)}, f32[256]{0:T(256)}, u32[]{:S(2)}) copy-start(f32[256]{0:T(256)} %copy-done.83) | copy-start | bytes 3076
  970.4 107.2 %copy-start.74 = (f32[1280]{0:T(1024)S(1)}, f32[1280]{0:T(1024)}, u32[]{:S(2)}) copy-start(f32[1280]{0:T(1024)} %get-tuple-element.92) | copy-start | bytes 15364
  970.4 107.2 %copy-start.75 = (f32[1280]{0:T(1024)S(1)}, f32[1280]{0:T(1024)}, u32[]{:S(2)}) copy-start(f32[1280]{0:T(1024)} %convert_reduce_fusion) | copy-start | bytes 15364
  970.4 107.2 %copy-start.77 = (f32[768]{0:T(1024)S(1)}, f32[768]{0:T(1024)}, u32[]{:S(2)}) copy-start(f32[768]{0:T(1024)} %get-tuple-element.88) | copy-start | bytes 9220
  970.4 107.2 %copy-start.78 = (f32[768]{0:T(1024)S(1)}, f32[768]{0:T(1024)}, u32[]{:S(2)}) copy-start(f32[768]{0:T(1024)} %get-tuple-element.95) | copy-start | bytes 9220
  970.4 107.2 %copy-start.79 = (f32[768]{0:T(1024)S(1)}, f32[768]{0:T(1024)}, u32[]{:S(2)}) copy-start(f32[768]{0:T(1024)} %convert_reduce_fusion.3) | copy-start | bytes 9220
  970.4 107.2 %copy-start.80 = (f32[768]{0:T(1024)S(1)}, f32[768]{0:T(1024)}, u32[]{:S(2)}) copy-start(f32[768]{0:T(1024)} %convert_reduce_fusion.5) | copy-start | bytes 9220
  970.4 107.2 %copy-start.81 = (f32[768]{0:T(1024)S(1)}, f32[768]{0:T(1024)}, u32[]{:S(2)}) copy-start(f32[768]{0:T(1024)} %get-tuple-element.96) | copy-start | bytes 9220
  970.5 107.2 %copy-start.82 = (f32[768]{0:T(1024)S(1)}, f32[768]{0:T(1024)}, u32[]{:S(2)}) copy-start(f32[768]{0:T(1024)} %get-tuple-element.90) | copy-start | bytes 9220
  970.5 107.2 %copy-start.91 = (f32[1280]{0:T(1024)S(1)}, f32[1280]{0:T(1024)}, u32[]{:S(2)}) copy-start(f32[1280]{0:T(1024)} %get-tuple-element.162) | copy-start | bytes 15364
  970.5 107.2 %copy-start.92 = (f32[2,192]{1,0:T(2,128)S(1)}, f32[2,192]{1,0:T(2,128)}, u32[]{:S(2)}) copy-start(f32[2,192]{1,0:T(2,128)} %pad_maximum_fusion.12) | copy-start | bytes 4612
  970.5 107.2 %copy-start.94 = (f32[768]{0:T(1024)S(1)}, f32[768]{0:T(1024)}, u32[]{:S(2)}) copy-start(f32[768]{0:T(1024)} %get-tuple-element.172) | copy-start | bytes 9220
  970.5 147.1 %copy-start.25 = (bf16[1,256,1280]{2,1,0:T(8,128)(2,1)S(1)}, bf16[1,256,1280]{2,1,0:T(8,128)(2,1)}, u32[]{:S(2)}) copy-start(bf16[1,256,1280]{2,1,0:T(8,128)(2,1)} %param.31) | copy-start | bytes 1966084
  970.5 147.1 %copy-start.86 = (f32[256]{0:T(256)S(1)}, f32[256]{0:T(256)}, u32[]{:S(2)}) copy-start(f32[256]{0:T(256)} %copy-done.85) | copy-start | bytes 3076
  (95 other events, 753.3 us)
Sparse Core Ops, SparseCore 0:
  52.3 36.4 all-gather.19
  91.0 53.6 all-gather.9
  146.6 30.2 all-gather.11
  179.0 35.2 reduce-scatter.33
  216.5 51.0 reduce-scatter.19
  269.4 23.7 all-gather.23
  295.2 50.0 all-gather.21
  347.3 22.9 all-gather.25
  372.2 32.8 all-gather.15
  407.0 88.2 all-gather.13
  497.2 31.8 all-gather.17
  531.2 35.2 reduce-scatter.37
  568.9 34.2 reduce-scatter.35
  605.3 75.4 reduce-scatter.23
  683.0 53.5 reduce-scatter.21
  739.6 33.3 reduce-scatter.47
  776.2 40.2 reduce-scatter.45
  818.8 35.2 reduce-scatter.39
  900.0 119.6 all-reduce.29
  1021.9 52.2 reduce-scatter.25
  1078.1 42.1 reduce-scatter.43
  1124.6 42.4 reduce-scatter.41
  1171.1 63.0 reduce-scatter.31
  1238.5 62.9 reduce-scatter.29
  1305.4 40.2 reduce-scatter.27
